TPU v7x, 128 devices: a whole 4x4x4 slice. The times are simulated.
128 devices in a mesh: sample: 8 (over y_hi, z), landmark: 16 (over y_lo, x, core).
Axes of the slice: x: 4, y: 4 (y_hi: 2, y_lo: 2; y = y_hi * 2 + y_lo), z: 4, core: 2. Of those that a mesh axis runs over, the one named last changes fastest.
Arguments:
- embeddings: bfloat16 [8192, 4096], P('sample'), may hold values from -6 to 6
- landmarks: bfloat16 [16384, 4096], P('landmark'), may hold values from -6 to 6
- factor: bfloat16 [16384, 16384], P('landmark', 'sample')
- flips: int32 [512, 8192], P(None, 'sample'), may hold values from 0 to 1
- labels: int32 [8192], P('sample'), may hold values from 0 to 1, as said below
- counts: int32 [8], replicated, may hold values from 256 to 1024, as said below
Outputs:
- whitened: bfloat16 [16384, 512], P(('sample', 'landmark'))
- statistic: float32 [512], replicated
Inputs may be any that keep to these rules, and one draw needn't show every extreme that they name: `counts`: one slab holds exactly 1024 live rows. `labels`: 0 or 1; the first slot of every slab is of corpus 0 and the second of corpus 1.
All inputs are finite; a program needn't handle non-finite values.
Results may differ from a plain program's by a relative error of at most 0.029.
Values may be sent and summed in bfloat16 or wider, within the bound.
A program may use at most 128 MiB of HBM per device.

v0:
```python
import math
import jax
import jax.numpy as jnp
from jax import lax
from jax.sharding import PartitionSpec as P

D = 4096
LANDMARKS = 16384


def whiten_maker(factor, moments_half):
    return lax.dot_general(
        factor, moments_half, (((0,), (1,)), ((), ())), preferred_element_type=jnp.float32
    )


def local(embeddings, landmarks, factor, flips, labels, counts):
    slot_count = embeddings.shape[0]
    slab_total = counts.shape[0]
    here_index = lax.axis_index("sample")
    own_count = jnp.sum(jnp.where(jnp.arange(slab_total, dtype=jnp.int32) == here_index, counts, 0))
    live_rows = (jnp.arange(slot_count, dtype=jnp.int32) < own_count).astype(jnp.float32)
    corpus = labels.astype(jnp.float32)
    count_a, count_b = lax.psum(
        (jnp.sum(live_rows * (1.0 - corpus)), jnp.sum(live_rows * corpus)), "sample"
    )
    balance = jnp.sqrt(count_a * count_b / (count_a + count_b))
    row_weight = live_rows * ((1.0 - corpus) / count_a - corpus / count_b) * balance
    wide_x = embeddings.astype(jnp.float32)
    row_scale = lax.rsqrt(jnp.mean(wide_x * wide_x, axis=1) + 1e-06)
    wide_z = landmarks.astype(jnp.float32)
    point_scale = lax.rsqrt(jnp.mean(wide_z * wide_z, axis=1) + 1e-06)
    signs = (2 * flips - 1).astype(jnp.bfloat16)
    cross = lax.dot_general(
        embeddings, landmarks, (((1,), (1,)), ((), ())), preferred_element_type=jnp.float32
    )
    kern = jnp.exp(0.5 * cross * row_scale[:, None] * point_scale[None, :] / math.sqrt(D))
    weighted = (row_weight[:, None] * kern).astype(jnp.bfloat16)
    partial_value = jnp.dot(signs, weighted, preferred_element_type=jnp.float32)
    summed = lax.psum(partial_value.astype(jnp.bfloat16), "sample")
    wide = lax.psum_scatter(
        whiten_maker(factor, summed).astype(jnp.bfloat16),
        "landmark",
        scatter_dimension=0,
        tiled=True,
    ).astype(jnp.float32)
    share = jnp.sum(wide * wide, axis=0)
    statistic = lax.psum(share, ("sample", "landmark")) / LANDMARKS
    return (wide.astype(jnp.bfloat16), statistic)


def solution(mesh):
    return jax.shard_map(
        local,
        mesh=mesh,
        in_specs=(
            P("sample", None),
            P("landmark", None),
            P("landmark", "sample"),
            P(None, "sample"),
            P("sample"),
            P(),
        ),
        out_specs=(P(("sample", "landmark"), None), P()),
        check_vma=False,
    )
```

profile of v0, /device:TPU:1, one launch (start us, length us, event | category | flops | bytes accessed | tf_op | source)
XLA Modules:
  0.0 293.1 jit_solution(10554155324927165992)
XLA Ops:
  7.2 0.0 all-reduce.3.cloned.1.call-start
  7.2 1.3 fusion.9
  8.5 2.0 select_reduce_fusion
  10.5 23.3 %all-reduce = (f32[]{:T(128)}, f32[]{:T(128)}) all-reduce(f32[]{:T(128)} %get-tuple-element.7, f32[]{:T(128)} %get-tuple-element.6), channel_id=1, replica_groups=mesh['sample'=8,'landmark'=16] {'sample'}, use_global_device_ids=true, to_apply=%region_2.3 | all-reduce | flops 2 | bytes 16 | tf_op jit(solution)/shard_map/psum | solution.py:24
  36.3 2.5 select_multiply_fusion
  38.9 0.0 copy-start
  38.9 5.2 %multiply_reduce_fusion.1 = f32[1024]{0:T(1024)S(1)} fusion(bf16[1024,4096]{1,0:T(8,128)(2,1)} %param.6), kind=kLoop, calls=%fused_computation.1 | loop fusion | flops 12581888 | bytes 8392704 | tf_op jit(solution)/shard_map/reduce_sum | solution.py:30
  44.1 0.5 copy-done
  44.7 0.0 copy-start.1
  44.7 1.7 multiply_reduce_fusion
  46.4 0.0 copy-done.1
  46.4 16.2 %fusion.6 = bf16[512,1024]{1,0:T(8,128)(2,1)} fusion(bf16[1024,4096]{1,0:T(8,128)(2,1)} %param.6, bf16[1024,4096]{1,0:T(8,128)(2,1)} %param.7, f32[1024]{0:T(1024)S(1)} %get-tuple-element.10, f32[1024]{0:T(1024)S(1)} %get-tuple-element.11, f32[1024]{0:T(1024)S(1)} %select_multiply_fusion, s32[512,1024]{1,0:T(8,128)S(1)} %copy-done.1), kind=kOutput, calls=%fused_computation.11 | convolution fusion | flops 9671016448 | bytes 19935232 | tf_op jit(solution)/shard_map/dot_general | solution.py:39
  62.6 0.0 all-reduce.3.cloned.1.call-update
  62.6 0.0 reduce-scatter.4.cloned.1.call-start
  62.7 83.6 %all-reduce.3.cloned.1.call-done = bf16[512,1024]{1,0:T(8,128)(2,1)} async-done(((bf16[512,1024]{1,0:T(8,128)(2,1)}), bf16[512,1024]{1,0:T(8,128)(2,1)}) %all-reduce.3.cloned.1.call-update) | async-done | bytes 1048592 | tf_op jit(solution)/shard_map/psum | solution.py:40
  146.3 4.8 %fusion = bf16[2048,512]{0,1:T(8,128)(2,1)S(1)} fusion(bf16[512,1024]{1,0:T(8,128)(2,1)} %all-reduce.3.cloned.1.call-done, bf16[1024,2048]{1,0:T(8,128)(2,1)} %param.8), kind=kOutput, calls=%fused_computation.4 | convolution fusion | flops 2148532224 | bytes 7340032 | tf_op jit(solution)/shard_map/dot_general | solution.py:12
  151.1 2.5 copy.10
  153.6 0.0 reduce-scatter.4.cloned.1.call-update
  153.7 62.8 %reduce-scatter.4.cloned.1.call-done = bf16[128,512]{1,0:T(8,128)(2,1)} async-done(((bf16[2048,512]{1,0:T(8,128)(2,1)}), bf16[128,512]{1,0:T(8,128)(2,1)}) %reduce-scatter.4.cloned.1.call-update) | async-done | bytes 131088
  216.4 1.0 copy.11
  217.4 0.2 multiply_reduce_fusion.2
  217.6 68.1 %psum.31 = f32[512]{0:T(512)S(1)} all-reduce(f32[512]{0:T(512)S(1)} %multiply_reduce_fusion.2), channel_id=1, replica_groups=mesh['sample'=8,'landmark'=16] {'sample','landmark'}, use_global_device_ids=true, to_apply=%region_10.11 | all-reduce | flops 512 | bytes 4096 | tf_op jit(solution)/shard_map/psum | solution.py:48
  285.7 0.6 broadcast_multiply_fusion
  (1 shorter events, 0.0 us)
Async XLA Ops:
  7.2 139.1 %all-reduce.3.cloned.1.call-start = ((), (), s32[]{:S(2)}) async-start(), calls=%async_computation.1 | async-start | bytes 2097152 | tf_op jit(solution)/shard_map/psum | solution.py:40
  38.9 5.8 %copy-start = (bf16[1024,4096]{1,0:T(8,128)(2,1)S(1)}, bf16[1024,4096]{1,0:T(8,128)(2,1)}, u32[]{:S(2)}) copy-start(bf16[1024,4096]{1,0:T(8,128)(2,1)} %param.7) | copy-start | bytes 25165828
  44.7 1.7 copy-start.1
  62.6 153.8 %reduce-scatter.4.cloned.1.call-start = ((), (), s32[]{:S(2)}) async-start(), calls=%async_computation.2 | async-start | bytes 2228224
Sparse Core Ops, SparseCore 0:
  62.7 83.4 all-reduce.2
  153.8 62.5 reduce-scatter.3
where the time goes:
time: 293 us
  waiting for transfers between devices  146 us (50%)
  blocking collectives  91.4 us (31%)
  matrix products  21.1 us (7%)
  between operations  16.6 us (6%)
  other arithmetic  13.5 us (5%)
  local copies, waits for them, and re-layouts  4.09 us (1%)
    psum x1, waiting for transfers between devices, local(): summed = lax.psum(partial_value.astype(jnp.bfloat16), 'sample')  83.6 us
    psum x1, blocking collectives, local(): statistic = lax.psum(share, ('sample', 'landmark')) / LANDMARKS  68.1 us
    unnamed x3, waiting for transfers between devices  62.8 us
    psum x1, blocking collectives, local(): lax.psum((jnp.sum(live_rows * (1.0 - corpus)), jnp.sum(live_rows * corpus...  23.3 us
    dot_general x1, matrix products, local(): partial_value = jnp.dot(signs, weighted, preferred_element_type=jnp.float32)  16.2 us
  transfers between devices with their start and end apart: 2, of which 2 were waited for; matrix products, arithmetic and copies ran while one was open for 0% of the time, Pallas kernels for 0%

commit v1 on v0

--- a/solution.py
+++ b/solution.py
@@ -1,11 +1,21 @@
+import functools
 import math
 import jax
 import jax.numpy as jnp
 from jax import lax
 from jax.sharding import PartitionSpec as P
+from jax.lax import psum
 
 D = 4096
 LANDMARKS = 16384
+
+
+def balance_sums_all(m, bus_axis, peer_axis):
+    passed = psum(psum(m, bus_axis), axis_name=peer_axis)
+    return passed
+
+
+samples_all_read = functools.partial(balance_sums_all, bus_axis="landmark", peer_axis="sample")
 
 
 def whiten_maker(factor, moments_half):
@@ -45,7 +55,7 @@
         tiled=True,
     ).astype(jnp.float32)
     share = jnp.sum(wide * wide, axis=0)
-    statistic = lax.psum(share, ("sample", "landmark")) / LANDMARKS
+    statistic = samples_all_read(share) / LANDMARKS
     return (wide.astype(jnp.bfloat16), statistic)
 
 

time: 293 us -> 280 us (0.956); the launches traced: 293 us -> 276 us
  blocking collectives: 91.4 us -> 74.4 us
    psum x1 -> x2, blocking collectives: 68.1 us -> 51.1 us  [balance_sums_all(): passed = psum(psum(m, bus_axis), axis_name=peer_axis)]
where the time goes in v1:
time: 280 us; the launch traced here: 276 us
  waiting for transfers between devices  146 us (52%)
  blocking collectives  74.4 us (27%)
  matrix products  21.1 us (8%)
  between operations  16.6 us (6%)
  other arithmetic  13.5 us (5%)
  local copies, waits for them, and re-layouts  4.09 us (1%)
    psum x1, waiting for transfers between devices, local(): summed = lax.psum(partial_value.astype(jnp.bfloat16), 'sample')  83.6 us
    unnamed x3, waiting for transfers between devices  62.8 us
    psum x2, blocking collectives, balance_sums_all(): passed = psum(psum(m, bus_axis), axis_name=peer_axis)  51.1 us
    psum x1, blocking collectives, local(): lax.psum((jnp.sum(live_rows * (1.0 - corpus)), jnp.sum(live_rows * corpus...  23.3 us
    dot_general x1, matrix products, local(): partial_value = jnp.dot(signs, weighted, preferred_element_type=jnp.float32)  16.2 us
  transfers between devices with their start and end apart: 2, of which 2 were waited for; matrix products, arithmetic and copies ran while one was open for 0% of the time, Pallas kernels for 0%

profile of v1, /device:TPU:1, one launch (start us, length us, event | category | flops | bytes accessed | tf_op | source)
XLA Modules:
  0.0 276.1 jit_solution(13844982850213343633)
XLA Ops:
  7.2 0.0 all-reduce.3.cloned.1.call-start
  7.2 1.3 fusion.9
  8.5 2.0 select_reduce_fusion
  10.5 23.3 %all-reduce = (f32[]{:T(128)}, f32[]{:T(128)}) all-reduce(f32[]{:T(128)} %get-tuple-element.7, f32[]{:T(128)} %get-tuple-element.6), channel_id=1, replica_groups=mesh['sample'=8,'landmark'=16] {'sample'}, use_global_device_ids=true, to_apply=%region_2.3 | all-reduce | flops 2 | bytes 16 | tf_op jit(solution)/shard_map/psum | solution.py:34
  36.3 2.5 select_multiply_fusion
  38.9 0.0 copy-start
  38.9 5.2 %multiply_reduce_fusion.1 = f32[1024]{0:T(1024)S(1)} fusion(bf16[1024,4096]{1,0:T(8,128)(2,1)} %param.6), kind=kLoop, calls=%fused_computation.1 | loop fusion | flops 12581888 | bytes 8392704 | tf_op jit(solution)/shard_map/reduce_sum | solution.py:40
  44.1 0.5 copy-done
  44.7 0.0 copy-start.1
  44.7 1.7 multiply_reduce_fusion
  46.4 0.0 copy-done.1
  46.4 16.2 %fusion.6 = bf16[512,1024]{1,0:T(8,128)(2,1)} fusion(bf16[1024,4096]{1,0:T(8,128)(2,1)} %param.6, bf16[1024,4096]{1,0:T(8,128)(2,1)} %param.7, f32[1024]{0:T(1024)S(1)} %get-tuple-element.10, f32[1024]{0:T(1024)S(1)} %get-tuple-element.11, f32[1024]{0:T(1024)S(1)} %select_multiply_fusion, s32[512,1024]{1,0:T(8,128)S(1)} %copy-done.1), kind=kOutput, calls=%fused_computation.11 | convolution fusion | flops 9671016448 | bytes 19935232 | tf_op jit(solution)/shard_map/dot_general | solution.py:49
  62.6 0.0 all-reduce.3.cloned.1.call-update
  62.6 0.0 reduce-scatter.4.cloned.1.call-start
  62.7 83.6 %all-reduce.3.cloned.1.call-done = bf16[512,1024]{1,0:T(8,128)(2,1)} async-done(((bf16[512,1024]{1,0:T(8,128)(2,1)}), bf16[512,1024]{1,0:T(8,128)(2,1)}) %all-reduce.3.cloned.1.call-update) | async-done | bytes 1048592 | tf_op jit(solution)/shard_map/psum | solution.py:50
  146.3 4.8 %fusion = bf16[2048,512]{0,1:T(8,128)(2,1)S(1)} fusion(bf16[512,1024]{1,0:T(8,128)(2,1)} %all-reduce.3.cloned.1.call-done, bf16[1024,2048]{1,0:T(8,128)(2,1)} %param.8), kind=kOutput, calls=%fused_computation.4 | convolution fusion | flops 2148532224 | bytes 7340032 | tf_op jit(solution)/shard_map/dot_general | solution.py:22
  151.1 2.5 copy.10
  153.6 0.0 reduce-scatter.4.cloned.1.call-update
  153.7 62.8 %reduce-scatter.4.cloned.1.call-done = bf16[128,512]{1,0:T(8,128)(2,1)} async-done(((bf16[2048,512]{1,0:T(8,128)(2,1)}), bf16[128,512]{1,0:T(8,128)(2,1)}) %reduce-scatter.4.cloned.1.call-update) | async-done | bytes 131088
  216.4 1.0 copy.11
  217.4 0.2 multiply_reduce_fusion.2
  217.6 30.8 %psum.38 = f32[512]{0:T(512)S(1)} all-reduce(f32[512]{0:T(512)S(1)} %multiply_reduce_fusion.2), channel_id=1, replica_groups=mesh['sample'=8,'landmark'=16] {'landmark'}, use_global_device_ids=true, to_apply=%region_10.11 | all-reduce | flops 512 | bytes 4096 | tf_op jit(solution)/shard_map/psum | solution.py:14
  248.4 20.2 %psum.39 = f32[512]{0:T(512)S(1)} all-reduce(f32[512]{0:T(512)S(1)} %psum.38), channel_id=1, replica_groups=mesh['sample'=8,'landmark'=16] {'sample'}, use_global_device_ids=true, to_apply=%region_11.12 | all-reduce | flops 512 | bytes 4096 | tf_op jit(solution)/shard_map/psum | solution.py:14
  268.7 0.6 broadcast_multiply_fusion
  (1 shorter events, 0.0 us)
Async XLA Ops:
  7.2 139.1 %all-reduce.3.cloned.1.call-start = ((), (), s32[]{:S(2)}) async-start(), calls=%async_computation.1 | async-start | bytes 2097152 | tf_op jit(solution)/shard_map/psum | solution.py:50
  38.9 5.8 %copy-start = (bf16[1024,4096]{1,0:T(8,128)(2,1)S(1)}, bf16[1024,4096]{1,0:T(8,128)(2,1)}, u32[]{:S(2)}) copy-start(bf16[1024,4096]{1,0:T(8,128)(2,1)} %param.7) | copy-start | bytes 25165828
  44.7 1.7 copy-start.1
  62.6 153.8 %reduce-scatter.4.cloned.1.call-start = ((), (), s32[]{:S(2)}) async-start(), calls=%async_computation.2 | async-start | bytes 2228224
Sparse Core Ops, SparseCore 0:
  62.7 83.4 all-reduce.2
  153.8 62.5 reduce-scatter.3
